TPU v7x, 256 devices: a whole 4x4x8 slice. The times are simulated.
256 devices in a mesh: edge: 64 (over y, z, core), pix: 4 (over x).
Axes of the slice: x: 4, y: 4, z: 8, core: 2. Of those that a mesh axis runs over, the one named last changes fastest.
Arguments:
- features: bfloat16 [128, 48, 64, 128], P('edge', 'pix'), may hold values from -6 to 6
- poses: float32 [128, 6], replicated, may hold values from -1.5 to 1.5
- inv_depth: float32 [128, 3072], P('edge', 'pix'), may hold values from 0.25 to 2
- hidden: bfloat16 [256, 48, 64, 128], P('edge', 'pix'), may hold values from -1 to 1
- edges: int32 [256, 2], P('edge'), may hold values from 0 to 127, as said below
- counts: int32 [64], P('edge'), may hold values from 1 to 4, 128 in all
- w_gates: bfloat16 [9, 256, 256], replicated, may hold values from -0.125 to 0.125
- w_cand: bfloat16 [9, 256, 128], replicated, may hold values from -0.125 to 0.125
- w_head: bfloat16 [4, 128], replicated, may hold values from -0.5 to 0.5
Outputs:
- hidden_out: bfloat16 [256, 48, 64, 128], P('edge', 'pix')
- pose_update: float32 [128, 6], P('edge')
- depth_update: float32 [128, 3072], P('edge', 'pix')
Inputs may be any that keep to these rules, and one draw needn't show every extreme that they name: `edges`: slot s lies on node n = s // 4; its source frame is 2n or 2n + 1 and its target is one of the frames 2n to 2n + 3 other than the source; on the last node the target is the other frame of its own pair. The first slot of node n goes from frame 2n to frame 2n + 2 (on the last node to 2n + 1). Dead slots hold such pairs too.
All inputs are finite; a program needn't handle non-finite values. No bound on the sum of `counts` on one device may be relied on, other than what follows from the above.
Results may differ from a plain program's by a relative error of at most 0.011.
Values may be sent and summed in bfloat16 or wider, within the bound.
No kernel may reach another device: no remote copies, remote signals or barrier semaphores. Data moves between devices by JAX's collectives and lax.ppermute only.
A program may use at most 192 MiB of HBM per device.

v0:
```python
import math
import jax
import jax.numpy as jnp
from jax import lax
from jax.sharding import PartitionSpec as P

PRECISE = lax.Precision.HIGHEST
POSE_DAMPING = 0.1
DEPTH_DAMPING = 0.1


def passed_along(value, axis, steps):
    count = lax.axis_size(axis)
    first, last = (max(0, -steps), min(count, count - steps))
    return lax.ppermute(value, axis, [(source, source + steps) for source in range(first, last)])


def padded_2(cells, sides, width):
    for axis, dim in sides:
        count = lax.axis_size(axis)
        ends = count - 1
        head = lax.slice_in_dim(cells, 0, width, axis=dim)
        tail = lax.slice_in_dim(cells, cells.shape[dim] - width, cells.shape[dim], axis=dim)
        cells = jnp.concatenate(
            [
                lax.ppermute(tail, axis, [(i, (i + 1) % count) for i in range(ends)]),
                cells,
                lax.ppermute(head, axis, [((i + 1) % count, i) for i in range(ends)]),
            ],
            axis=dim,
        )
    return cells


def pixel_coords(row_start, row_count, total_rows, col_count):
    row_ids = (row_start + lax.broadcasted_iota(jnp.int32, (row_count, col_count), 0)).astype(
        jnp.float32
    )
    col_ids = lax.broadcasted_iota(jnp.int32, (row_count, col_count), 1).astype(jnp.float32)
    half_width = col_count / 2.0
    horizontal = (col_ids - (col_count - 1) / 2.0) / half_width
    vertical = (row_ids - (total_rows - 1) / 2.0) / half_width
    return (horizontal.reshape(-1), vertical.reshape(-1))


def match_rows(queries, targets, factor):
    scores = jnp.einsum("pc,qc->pq", queries, targets, preferred_element_type=jnp.float32) * factor
    row_max = jnp.max(scores, axis=1, keepdims=True)
    weights = jnp.exp(scores - row_max)
    row_total = jnp.sum(weights, axis=1, keepdims=True)
    weighted_sum = jnp.dot(
        weights.astype(jnp.bfloat16), targets, preferred_element_type=jnp.float32
    )
    return (weighted_sum / row_total).astype(jnp.bfloat16)


def conv_taps(framed, weight, row_count, col_count):
    padded = jnp.pad(framed, ((0, 0), (0, 0), (1, 1), (0, 0)))
    result = None
    for tap_index in range(9):
        row_off = tap_index // 3
        col_off = tap_index % 3
        window = padded[:, row_off : row_off + row_count, col_off : col_off + col_count, :]
        tap_term = jnp.einsum(
            "srwc,cd->srwd", window, weight[tap_index], preferred_element_type=jnp.float32
        )
        result = tap_term if tap_index == 0 else result + tap_term
    return result


def bundle_terms(head_out, live_mask, inv_rho, xi_rel, src_local, tgt_local, horizontal, vertical):
    flow_pred = head_out[:, 0:2]
    confidence = jax.nn.sigmoid(head_out[:, 2:4]) * live_mask[:, None, None]
    unit_row = jnp.ones_like(inv_rho)
    zero_row = jnp.zeros_like(inv_rho)
    horiz_row = horizontal[None, :] * unit_row
    vert_row = vertical[None, :] * unit_row
    jacobian_horiz = jnp.stack(
        [
            inv_rho,
            zero_row,
            -horiz_row * inv_rho,
            -horiz_row * vert_row,
            1.0 + horiz_row * horiz_row,
            -vert_row,
        ],
        axis=1,
    )
    jacobian_vert = jnp.stack(
        [
            zero_row,
            inv_rho,
            -vert_row * inv_rho,
            -(1.0 + vert_row * vert_row),
            horiz_row * vert_row,
            horiz_row,
        ],
        axis=1,
    )
    jacobian = jnp.stack([jacobian_horiz, jacobian_vert], axis=1)
    predicted = jnp.einsum("skjp,sj->skp", jacobian, xi_rel, precision=PRECISE)
    residual = flow_pred - predicted
    forward_shift = xi_rel[:, 2:3]
    depth_jacobian = jnp.stack(
        [xi_rel[:, 0:1] - horiz_row * forward_shift, xi_rel[:, 1:2] - vert_row * forward_shift],
        axis=1,
    )
    frame_ids = jnp.arange(4, dtype=jnp.int32)
    select = (tgt_local[:, None] == frame_ids[None, :]).astype(jnp.float32) - (
        src_local[:, None] == frame_ids[None, :]
    ).astype(jnp.float32)
    slot_count, pix_count = inv_rho.shape
    pose_jacobian = (select[:, None, :, None, None] * jacobian[:, :, None, :, :]).reshape(
        slot_count, 2, 24, pix_count
    )
    weighted = pose_jacobian * confidence[:, :, None, :]
    pose_pose = jnp.einsum("skip,skjp->ij", weighted, pose_jacobian, precision=PRECISE)
    pose_rhs = jnp.einsum("skip,skp->i", weighted, residual, precision=PRECISE)
    pose_depth_slot = jnp.einsum("skip,skp->sip", weighted, depth_jacobian, precision=PRECISE)
    depth_depth_slot = jnp.sum(confidence * depth_jacobian * depth_jacobian, axis=1)
    depth_rhs_slot = jnp.sum(confidence * depth_jacobian * residual, axis=1)
    source_pick = (src_local[:, None] == frame_ids[None, 0:2]).astype(jnp.float32)
    pose_depth = jnp.einsum("sf,sip->fip", source_pick, pose_depth_slot, precision=PRECISE)
    depth_depth = DEPTH_DAMPING + jnp.einsum(
        "sf,sp->fp", source_pick, depth_depth_slot, precision=PRECISE
    )
    depth_rhs = jnp.einsum("sf,sp->fp", source_pick, depth_rhs_slot, precision=PRECISE)
    depth_ratio = pose_depth / depth_depth[:, None, :]
    reduced = pose_pose - jnp.einsum("fip,fjp->ij", depth_ratio, pose_depth, precision=PRECISE)
    reduced_rhs = pose_rhs - jnp.einsum("fip,fp->i", depth_ratio, depth_rhs, precision=PRECISE)
    return (reduced, reduced_rhs, pose_depth, depth_depth, depth_rhs)


def factor_solve(factor_low, rhs_mat):
    lower_part = lax.linalg.triangular_solve(factor_low, rhs_mat, left_side=True, lower=True)
    return lax.linalg.triangular_solve(
        factor_low, lower_part, left_side=True, lower=True, transpose_a=True
    )


def sweep_nodes(blocks, vectors):
    node_total = blocks.shape[0]
    node_ids = jnp.arange(node_total, dtype=jnp.int32)
    same_node = (node_ids[:, None] == node_ids[None, :]).astype(jnp.float32)
    next_node = (node_ids[None, :] == node_ids[:, None] + 1).astype(jnp.float32)
    previous_far = jnp.concatenate(
        [jnp.zeros((1, 12, 12), jnp.float32), blocks[:-1, 12:, 12:]], axis=0
    )
    diag_blocks = blocks[:, :12, :12] + previous_far
    link_blocks = blocks[:, :12, 12:]
    dense = jnp.einsum("nm,nij->nimj", same_node, diag_blocks, precision=PRECISE)
    upper = jnp.einsum("nm,nij->nimj", next_node, link_blocks, precision=PRECISE)
    dense = dense + upper + jnp.transpose(upper, (2, 3, 0, 1))
    system_size = 12 * node_total
    system = dense.reshape(system_size, system_size) + POSE_DAMPING * jnp.eye(
        system_size, dtype=jnp.float32
    )
    previous_rhs = jnp.concatenate([jnp.zeros((1, 12), jnp.float32), vectors[:-1, 12:]], axis=0)
    system_rhs = (vectors[:, :12] + previous_rhs).reshape(system_size)
    factor_low = jnp.linalg.cholesky(system)
    solution = factor_solve(factor_low, system_rhs[:, None])[:, 0]
    return solution.reshape(node_total, 12)


def shards(features, poses, inv_depth, hidden, edges, counts, w_gates, w_cand, w_head):
    slot_count, row_count, col_count, hid_width = hidden.shape
    channels = features.shape[3]
    frame_count = poses.shape[0]
    node_rank = lax.axis_index("edge")
    base_frame = 2 * node_rank
    pix_rank = lax.axis_index("pix")
    total_rows = row_count * lax.axis_size("pix")
    local_pixels = row_count * col_count
    own_whole = lax.all_gather(features, "pix", axis=1, tiled=True)
    next_whole = passed_along(own_whole, "edge", -1)
    nearby = jnp.concatenate([own_whole, next_whole], axis=0)
    nearby = nearby.reshape(4, total_rows * col_count, channels)
    own_flat = features.reshape(2, local_pixels, channels)
    src_local = edges[:, 0] - base_frame
    tgt_local = edges[:, 1] - base_frame
    factor = 2.0 / math.sqrt(channels)
    matched_list = []
    for slot_index in range(slot_count):
        queries = lax.dynamic_index_in_dim(own_flat, src_local[slot_index], 0, keepdims=False)
        targets = lax.dynamic_index_in_dim(nearby, tgt_local[slot_index], 0, keepdims=False)
        matched_list.append(match_rows(queries, targets, factor))
    matched = jnp.stack(matched_list, axis=0).reshape(slot_count, row_count, col_count, channels)
    inputs = jnp.concatenate([hidden, matched], axis=3)
    state_wide = hidden.astype(jnp.float32)
    framed = padded_2(inputs, (("pix", 1),), 1)
    gates = jax.nn.sigmoid(conv_taps(framed, w_gates, row_count, col_count))
    update = gates[..., :hid_width]
    reset_state = (gates[..., hid_width:] * state_wide).astype(jnp.bfloat16)
    reset_framed = padded_2(reset_state, (("pix", 1),), 1)
    second = jnp.concatenate([reset_framed, framed[..., hid_width:]], axis=3)
    candidate = jnp.tanh(conv_taps(second, w_cand, row_count, col_count))
    fresh = ((1.0 - update) * state_wide + update * candidate).astype(jnp.bfloat16)
    live_mask = (lax.broadcasted_iota(jnp.int32, (slot_count,), 0) < counts[0]).astype(jnp.float32)
    hidden_out = jnp.where(live_mask[:, None, None, None] > 0.5, fresh, hidden)
    head_out = jnp.einsum(
        "kc,spc->skp",
        w_head,
        fresh.reshape(slot_count, local_pixels, hid_width),
        preferred_element_type=jnp.float32,
    )
    pair_ids = jnp.arange(2, dtype=jnp.int32)
    source_pick = (src_local[:, None] == pair_ids[None, :]).astype(jnp.float32)
    inv_rho = jnp.dot(source_pick, inv_depth, precision=PRECISE)
    all_ids = jnp.arange(frame_count, dtype=jnp.int32)
    frame_diff = (edges[:, 1:2] == all_ids[None, :]).astype(jnp.float32) - (
        edges[:, 0:1] == all_ids[None, :]
    ).astype(jnp.float32)
    xi_rel = jnp.dot(frame_diff, poses, precision=PRECISE)
    horizontal, vertical = pixel_coords(pix_rank * row_count, row_count, total_rows, col_count)
    reduced_part, rhs_part, pose_depth, depth_depth, depth_rhs = bundle_terms(
        head_out, live_mask, inv_rho, xi_rel, src_local, tgt_local, horizontal, vertical
    )
    reduced, reduced_rhs = lax.psum((reduced_part, rhs_part), "pix")
    blocks, vectors = (
        lax.all_gather(reduced[None], "edge", axis=0, tiled=True),
        lax.all_gather(reduced_rhs[None], "edge", axis=0, tiled=True),
    )
    values = sweep_nodes(blocks, vectors)
    node_total = values.shape[0]
    node_pose = lax.dynamic_index_in_dim(values, node_rank, 0, keepdims=False)
    after_index = jnp.minimum(node_rank + 1, node_total - 1)
    next_pose = lax.dynamic_index_in_dim(values, after_index, 0, keepdims=False) * (
        node_rank + 1 < node_total
    ).astype(jnp.float32)
    pose_update = node_pose.reshape(2, 6)
    pose_pair = jnp.concatenate([node_pose, next_pose], axis=0)
    depth_update = (
        depth_rhs - jnp.einsum("fip,i->fp", pose_depth, pose_pair, precision=PRECISE)
    ) / depth_depth
    return (hidden_out, pose_update, depth_update)


def solution(mesh):
    placed = (
        P("edge", "pix", None, None),
        P(),
        P("edge", "pix"),
        P("edge", "pix", None, None),
        P("edge", None),
        P("edge"),
        P(),
        P(),
        P(),
    )
    return jax.shard_map(
        shards,
        mesh=mesh,
        in_specs=placed,
        out_specs=(P("edge", "pix", None, None), P("edge", None), P("edge", "pix")),
        check_vma=False,
    )
```

profile of v0, /device:TPU:1, one launch (start us, length us, event | category | flops | bytes accessed | tf_op | source)
XLA Modules:
  0.0 581.9 jit_solution(17546545287537749910)
XLA Ops:
  22.5 20.2 %all-gather.3.cloned.1.call-done = bf16[2,48,64,128]{3,2,1,0:T(8,128)(2,1)} async-done(((bf16[2,12,64,128]{3,2,1,0:T(8,128)(2,1)}), bf16[2,48,64,128]{3,2,1,0:T(8,128)(2,1)}) %all-gather.3.cloned.1.call-update) | async-done | bytes 1572880 | tf_op jit(solution)/shard_map/all_gather | solution.py:174
  42.7 2.6 collective-permute-start
  51.2 13.6 %collective-permute-done = bf16[2,48,64,128]{3,2,1,0:T(8,128)(2,1)S(1)} collective-permute-done((bf16[2,48,64,128]{3,2,1,0:T(8,128)(2,1)}, bf16[2,48,64,128]{3,2,1,0:T(8,128)(2,1)S(1)}, u32[]{:S(2)}, u32[]{:S(2)}) %collective-permute-start) | collective-permute-done | bytes 1572896 | tf_op jit(solution)/shard_map/ppermute | solution.py:15
  64.7 1.7 pad_maximum_fusion
  69.6 2.3 fusion.137
  75.0 2.1 fusion.131
  80.2 2.3 fusion.125
  85.7 2.1 fusion.119
  89.2 4.0 collective-permute-start.1
  93.2 2.3 fusion.46
  98.7 2.2 fusion.31
  101.0 2.3 fusion.19
  103.2 4.9 add_divide_fusion
  109.7 4.4 collective-permute-start.3
  120.0 2.3 broadcast_select_fusion
  126.7 13.3 %all-reduce.5 = (f32[1,24,24]{2,1,0:T(8,128)S(1)}, f32[1,24]{1,0:T(1,128)S(1)}) all-reduce(f32[1,24,24]{2,1,0:T(8,128)S(1)} %fusion.97, f32[1,24]{1,0:T(1,128)S(1)} %fusion.106), channel_id=1, replica_groups=mesh['edge'=64,'pix'=4] {'pix'}, use_global_device_ids=true, to_apply=%region_9.10 | all-reduce | flops 600 | bytes 4800 | tf_op jit(solution)/shard_map/psum | solution.py:218
  139.9 58.5 %all_gather.10 = f32[64,24,24]{2,1,0:T(8,128)S(1)} all-gather(f32[1,24,24]{2,1,0:T(8,128)S(1)} %get-tuple-element.36), channel_id=1, replica_groups=mesh['edge'=64,'pix'=4] {'edge'}, dimensions={0}, use_global_device_ids=true | all-gather | bytes 149760 | tf_op jit(solution)/shard_map/all_gather | solution.py:220
  200.0 12.3 %fusion = f32[64,12,64,12]{1,0,3,2:T(8,128)} fusion(f32[64,64]{0,1:T(8,128)S(1)} %get-tuple-element.125, f32[64,12,12]{1,0,2:T(8,128)S(1)} %copy.62, f32[64,64]{0,1:T(8,128)S(1)} %get-tuple-element.124, f32[64,12,12]{1,0,2:T(8,128)S(1)} %copy.61), kind=kLoop, calls=%fused_computation.4 | loop fusion | flops 1769472 | bytes 2465792 | tf_op jit(solution)/shard_map/add | solution.py:153
  212.3 33.5 %copy.63 = f32[64,12,64,12]{3,2,1,0:T(8,128)} copy(f32[64,12,64,12]{1,0,3,2:T(8,128)} %fusion) | data formatting | bytes 4718592 | tf_op jit(solution)/shard_map/add | solution.py:153
  245.9 18.1 %fusion.1 = f32[64,12,64,12]{3,2,1,0:T(8,128)} fusion(f32[64,12,64,12]{3,2,1,0:T(8,128)} %copy.63, f32[64,64]{0,1:T(8,128)S(1)} %get-tuple-element.125, f32[64,12,12]{1,0,2:T(8,128)S(1)} %copy.62), kind=kLoop, calls=%fused_computation.5 | loop fusion | flops 1179648 | bytes 4771840 | tf_op jit(solution)/shard_map/add | solution.py:153
  264.0 22.7 %reshape.435 = f32[768,768]{1,0:T(8,128)} reshape(f32[64,12,64,12]{3,2,1,0:T(8,128)} %fusion.1) | data formatting | bytes 4718592 | tf_op jit(solution)/shard_map/reshape | solution.py:155
  286.6 2.0 copy.64
  290.3 3.2 copy.65
  293.5 2.1 fusion.18
  297.0 11.7 %cholesky.164 = f32[128,128]{1,0:T(8,128)S(1)} custom-call(f32[128,128]{1,0:T(8,128)S(1)} %cholesky.421), custom_call_target="Cholesky" | custom-call | tf_op jit(solution)/shard_map/jit(cholesky)/cholesky | solution.py:160
  308.9 9.8 %custom-call.48 = f32[1,128,128]{1,2,0:T(8,128)S(1)} custom-call(f32[1,128,128]{2,1,0:T(8,128)S(1)} %get-tuple-element.60), custom_call_target="InvertDiagBlocksLowerTriangular" | custom-call | tf_op jit(solution)/shard_map/jit(cholesky)/cholesky | solution.py:160
  321.7 11.7 %cholesky.187 = f32[128,128]{1,0:T(8,128)S(1)} custom-call(f32[128,128]{1,0:T(8,128)S(1)} %cholesky.425), custom_call_target="Cholesky" | custom-call | tf_op jit(solution)/shard_map/jit(cholesky)/cholesky | solution.py:160
  333.5 10.2 %custom-call.49 = f32[1,128,128]{1,2,0:T(8,128)S(1)} custom-call(f32[1,128,128]{2,1,0:T(8,128)S(1)} %get-tuple-element.58), custom_call_target="InvertDiagBlocksLowerTriangular" | custom-call | tf_op jit(solution)/shard_map/jit(cholesky)/cholesky | solution.py:160
  344.4 2.0 convolution_subtract_fusion.1
  346.3 11.7 %cholesky.352 = f32[128,128]{1,0:T(8,128)S(1)} custom-call(f32[128,128]{1,0:T(8,128)S(1)} %cholesky.430), custom_call_target="Cholesky" | custom-call | tf_op jit(solution)/shard_map/jit(cholesky)/cholesky | solution.py:160
  358.2 9.8 %custom-call.50 = f32[1,128,128]{1,2,0:T(8,128)S(1)} custom-call(f32[1,128,128]{2,1,0:T(8,128)S(1)} %get-tuple-element.56), custom_call_target="InvertDiagBlocksLowerTriangular" | custom-call | tf_op jit(solution)/shard_map/jit(cholesky)/cholesky | solution.py:160
  368.4 2.1 convolution_subtract_fusion.2
  370.5 11.9 %cholesky.371 = f32[128,128]{1,0:T(8,128)S(1)} custom-call(f32[128,128]{1,0:T(8,128)S(1)} %cholesky.435), custom_call_target="Cholesky" | custom-call | tf_op jit(solution)/shard_map/jit(cholesky)/cholesky | solution.py:160
  382.6 9.8 %custom-call.51 = f32[1,128,128]{1,2,0:T(8,128)S(1)} custom-call(f32[1,128,128]{2,1,0:T(8,128)S(1)} %get-tuple-element.54), custom_call_target="InvertDiagBlocksLowerTriangular" | custom-call | tf_op jit(solution)/shard_map/jit(cholesky)/cholesky | solution.py:160
  392.7 1.9 convolution_subtract_fusion.3
  394.6 11.7 %cholesky.390 = f32[128,128]{1,0:T(8,128)S(1)} custom-call(f32[128,128]{1,0:T(8,128)S(1)} %cholesky.440), custom_call_target="Cholesky" | custom-call | tf_op jit(solution)/shard_map/jit(cholesky)/cholesky | solution.py:160
  406.5 9.8 %custom-call.52 = f32[1,128,128]{1,2,0:T(8,128)S(1)} custom-call(f32[1,128,128]{2,1,0:T(8,128)S(1)} %get-tuple-element.52), custom_call_target="InvertDiagBlocksLowerTriangular" | custom-call | tf_op jit(solution)/shard_map/jit(cholesky)/cholesky | solution.py:160
  416.6 1.8 convolution_subtract_fusion.4
  418.4 11.7 %cholesky.408 = f32[128,128]{1,0:T(8,128)S(1)} custom-call(f32[128,128]{1,0:T(8,128)S(1)} %convolution_subtract_fusion.4), custom_call_target="Cholesky" | custom-call | tf_op jit(solution)/shard_map/jit(cholesky)/cholesky | solution.py:160
  434.2 37.7 %all-gather = f32[64,1,24]{2,1,0:T(1,128)S(1)} all-gather(f32[1,1,24]{2,1,0:T(1,128)S(1)} %bitcast.562), channel_id=1, replica_groups=mesh['edge'=64,'pix'=4] {'edge'}, dimensions={0}, use_global_device_ids=true | all-gather | bytes 6240 | tf_op jit(solution)/shard_map/all_gather | solution.py:221
  477.5 21.6 %while.1 = (s32[]{:T(128)}, f32[768,768]{0,1:T(8,128)}, s32[6,2]{0,1:T(2,128)S(1)}, f32[6,128,128]{2,1,0:T(8,128)}, s32[]{:T(128)}) while((s32[]{:T(128)}, f32[768,768]{0,1:T(8,128)}, s32[6,2]{0,1:T(2,128)S(1)}, f32[6,128,128]{2,1,0:T(8,128)}, s32[]{:T(128)}) %tuple.82), condition=%wide.while_cond, body=%wide.while_body.sunk | while | flops 2 | bytes 393329 | solution.py:136
  478.1 2.3 dynamic-slice.7
  481.7 2.3 dynamic-slice.7
  485.3 2.3 dynamic-slice.7
  488.9 2.3 dynamic-slice.7
  492.5 2.3 dynamic-slice.7
  496.1 2.2 dynamic-slice.7
  499.1 59.8 %custom-call.53 = f32[6,128,128]{1,2,0:T(8,128)S(1)} custom-call(f32[6,128,128]{2,1,0:T(8,128)} %get-tuple-element.10), custom_call_target="InvertDiagBlocksLowerTriangular" | custom-call | tf_op jit(solution)/shard_map/triangular_solve | solution.py:136
  (207 shorter events, 73.5 us)
Async XLA Ops:
  7.2 15.0 %copy-start = (f32[2,768]{1,0:T(2,128)S(1)}, f32[2,768]{1,0:T(2,128)}, u32[]{:S(2)}) copy-start(f32[2,768]{1,0:T(2,128)} %param.11) | copy-start | bytes 18436
  7.2 35.5 %all-gather.3.cloned.1.call-start = ((), (), s32[]{:S(2)}) async-start(), calls=%async_computation | async-start | bytes 1966080 | tf_op jit(solution)/shard_map/all_gather | solution.py:174
  42.7 22.0 %collective-permute-start = (bf16[2,48,64,128]{3,2,1,0:T(8,128)(2,1)}, bf16[2,48,64,128]{3,2,1,0:T(8,128)(2,1)S(1)}, u32[]{:S(2)}, u32[]{:S(2)}) collective-permute-start(bf16[2,48,64,128]{3,2,1,0:T(8,128)(2,1)} %all-gather.3.cloned.1.call-done), channel_id=1, source_target_pairs={{4,0},{8,4},{12,8},{16,12},{20,16},{24,20},{28,24},{32,28},{36,32}... | collective-permute-start | bytes 4718600 | tf_op jit(solution)/shard_map/ppermute | solution.py:15
  51.2 15.3 %copy-start.4 = (bf16[2,12,64,128]{3,2,1,0:T(8,128)(2,1)S(1)}, bf16[2,12,64,128]{3,2,1,0:T(8,128)(2,1)}, u32[]{:S(2)}) copy-start(bf16[2,12,64,128]{3,2,1,0:T(8,128)(2,1)} %param.9) | copy-start | bytes 1179652
  85.7 2.1 copy-start.2
  85.7 7.5 %copy-start.5 = (bf16[9,256,256]{2,1,0:T(8,128)(2,1)S(1)}, bf16[9,256,256]{2,1,0:T(8,128)(2,1)}, u32[]{:S(2)}) copy-start(bf16[9,256,256]{2,1,0:T(8,128)(2,1)} %param.15) | copy-start | bytes 3538948
  87.9 7.6 %collective-permute-start.2 = (bf16[4,1,64,256]{3,2,1,0:T(8,128)(2,1)S(1)}, bf16[4,1,64,256]{3,2,1,0:T(8,128)(2,1)S(1)}, u32[]{:S(2)}, u32[]{:S(2)}) collective-permute-start(bf16[4,1,64,256]{3,2,1,0:T(8,128)(2,1)S(1)} %get-tuple-element.45), channel_id=1, source_target_pairs={{1,0},{2,1},{3,2},{5,4},{6,5},{7,6},{9,8},{10,9},{11,10},{13,12},{... | collective-permute-start | bytes 393224 | tf_op jit(solution)/shard_map/ppermute | solution.py:28
  89.2 6.3 %collective-permute-start.1 = (bf16[4,1,64,256]{3,2,1,0:T(8,128)(2,1)S(1)}, bf16[4,1,64,256]{3,2,1,0:T(8,128)(2,1)S(1)}, u32[]{:S(2)}, u32[]{:S(2)}) collective-permute-start(bf16[4,1,64,256]{3,2,1,0:T(8,128)(2,1)S(1)} %get-tuple-element.44), channel_id=1, source_target_pairs={{0,1},{1,2},{2,3},{4,5},{5,6},{6,7},{8,9},{9,10},{10,11},{12,13},{... | collective-permute-start | bytes 393224 | tf_op jit(solution)/shard_map/ppermute | solution.py:26
  108.4 6.0 %collective-permute-start.4 = (bf16[4,1,64,128]{3,2,1,0:T(8,128)(2,1)S(1)}, bf16[4,1,64,128]{3,2,1,0:T(8,128)(2,1)S(1)}, u32[]{:S(2)}, u32[]{:S(2)}) collective-permute-start(bf16[4,1,64,128]{3,2,1,0:T(8,128)(2,1)S(1)} %get-tuple-element.49), channel_id=1, source_target_pairs={{1,0},{2,1},{3,2},{5,4},{6,5},{7,6},{9,8},{10,9},{11,10},{13,12},{... | collective-permute-start | bytes 196616 | tf_op jit(solution)/shard_map/ppermute | solution.py:28
  109.7 5.4 collective-permute-start.3
  114.2 1.2 copy-start.6
  120.0 2.3 copy-start.7
  295.6 1.4 copy-start.3
  477.5 97.4 %copy-start.1 = (f32[2,768]{1,0:T(2,128)S(1)}, f32[2,768]{1,0:T(2,128)}, u32[]{:S(2)}) copy-start(f32[2,768]{1,0:T(2,128)} %param.11) | copy-start | bytes 18436
Sparse Core Ops, SparseCore 0:
  9.8 32.8 all-gather.2
where the time goes:
time: 588 us; the launch traced here: 582 us
  other arithmetic  232 us (39%)
  blocking collectives  109 us (19%)
  local copies, waits for them, and re-layouts  89.6 us (15%)
  matrix products  66.9 us (11%)
  waiting for transfers between devices  35.2 us (6%)
  between operations  34.7 us (6%)
  starting transfers between devices  13.6 us (2%)
    another operation x23, other arithmetic, sweep_nodes(): factor_low = jnp.linalg.cholesky(system)  124 us
    another operation x4, other arithmetic, factor_solve(): lax.linalg.triangular_solve(factor_low, lower_part, left_side=True, lower...  61.4 us
    all_gather x1, blocking collectives, shards(): lax.all_gather(reduced[None], 'edge', axis=0, tiled=True)  58.5 us
    all_gather x1, blocking collectives, shards(): lax.all_gather(reduced_rhs[None], 'edge', axis=0, tiled=True)  37.7 us
    add x1, local copies, waits for them, and re-layouts, sweep_nodes(): dense = dense + upper + jnp.transpose(upper, (2, 3, 0, 1))  33.5 us
    add x2, other arithmetic, sweep_nodes(): dense = dense + upper + jnp.transpose(upper, (2, 3, 0, 1))  30.4 us
    reshape x2, local copies, waits for them, and re-layouts, sweep_nodes(): dense.reshape(system_size, system_size)  24.7 us
    another operation x30, local copies, waits for them, and re-layouts  21.5 us
  transfers between devices with their start and end apart: 6, of which 3 were waited for; matrix products, arithmetic and copies ran while one was open for 1% of the time, Pallas kernels for 0%

commit v1 on v0

--- a/solution.py
+++ b/solution.py
@@ -7,6 +7,27 @@
 PRECISE = lax.Precision.HIGHEST
 POSE_DAMPING = 0.1
 DEPTH_DAMPING = 0.1
+
+
+def collect(x, axis, dim):
+    size, position, rows = (lax.axis_size(axis), lax.axis_index(axis), x.shape[dim])
+    ahead = [(i, (i + 1) % size) for i in range(size)]
+    left = [(i, (i - 1) % size) for i in range(size)]
+    whole = jnp.zeros((*x.shape[:dim], size * rows, *x.shape[dim + 1 :]), x.dtype)
+    whole = lax.dynamic_update_slice_in_dim(whole, x, position * rows, axis=dim)
+    from_left = from_right = x
+    halfway = size // 2
+    for turn in range(1, halfway + 1):
+        from_left = lax.ppermute(from_left, axis, ahead)
+        whole = lax.dynamic_update_slice_in_dim(
+            whole, from_left, (position - turn) % size * rows, axis=dim
+        )
+        if turn < size - halfway:
+            from_right = lax.ppermute(from_right, axis, left)
+            whole = lax.dynamic_update_slice_in_dim(
+                whole, from_right, (position + turn) % size * rows, axis=dim
+            )
+    return whole
 
 
 def passed_along(value, axis, steps):
@@ -171,7 +192,7 @@
     pix_rank = lax.axis_index("pix")
     total_rows = row_count * lax.axis_size("pix")
     local_pixels = row_count * col_count
-    own_whole = lax.all_gather(features, "pix", axis=1, tiled=True)
+    own_whole = collect(features, "pix", 1)
     next_whole = passed_along(own_whole, "edge", -1)
     nearby = jnp.concatenate([own_whole, next_whole], axis=0)
     nearby = nearby.reshape(4, total_rows * col_count, channels)

time: 588 us -> 568 us (0.966)
  waiting for transfers between devices: 35.2 us -> 16 us
  between operations: 34.7 us -> 21.4 us
  starting transfers between devices: 13.6 us -> 20.4 us
    all_gather x1 -> x0, waiting for transfers between devices: 20.2 us -> none  [shards(): own_whole = lax.all_gather(features, 'pix', axis=1, tiled=True)]
  transfers between devices with their start and end apart: 6 -> 8, of which waited for: 3 -> 3; matrix products, arithmetic and copies ran while one was open for 1% -> 2% of each run, Pallas kernels for 0% -> 0%
where the time goes in v1:
time: 568 us; the launch traced here: 561 us
  other arithmetic  234 us (41%)
  blocking collectives  111 us (20%)
  local copies, waits for them, and re-layouts  90.3 us (16%)
  matrix products  66.9 us (12%)
  between operations  21.4 us (4%)
  starting transfers between devices  20.4 us (4%)
  waiting for transfers between devices  16 us (3%)
    another operation x23, other arithmetic, sweep_nodes(): factor_low = jnp.linalg.cholesky(system)  124 us
    another operation x4, other arithmetic, factor_solve(): lax.linalg.triangular_solve(factor_low, lower_part, left_side=True, lower...  61.9 us
    all_gather x1, blocking collectives, shards(): lax.all_gather(reduced[None], 'edge', axis=0, tiled=True)  59.8 us
    all_gather x1, blocking collectives, shards(): lax.all_gather(reduced_rhs[None], 'edge', axis=0, tiled=True)  37.3 us
    add x1, local copies, waits for them, and re-layouts, sweep_nodes(): dense = dense + upper + jnp.transpose(upper, (2, 3, 0, 1))  33.5 us
    add x2, other arithmetic, sweep_nodes(): dense = dense + upper + jnp.transpose(upper, (2, 3, 0, 1))  30.4 us
    reshape x2, local copies, waits for them, and re-layouts, sweep_nodes(): dense.reshape(system_size, system_size)  24.7 us
    another operation x30, local copies, waits for them, and re-layouts  21.5 us
  transfers between devices with their start and end apart: 8, of which 3 were waited for; matrix products, arithmetic and copies ran while one was open for 2% of the time, Pallas kernels for 0%

profile of v1, /device:TPU:1, one launch (start us, length us, event | category | flops | bytes accessed | tf_op | source)
XLA Modules:
  0.0 560.6 jit_solution(17116668057972166169)
XLA Ops:
  0.7 2.1 collective-permute-start
  7.7 3.0 collective-permute-done
  10.8 1.9 collective-permute-start.2
  24.4 4.0 collective-permute-start.3
  35.9 12.2 %collective-permute-done.3 = bf16[2,48,64,128]{3,2,1,0:T(8,128)(2,1)} collective-permute-done((bf16[2,48,64,128]{3,2,1,0:T(8,128)(2,1)S(1)}, bf16[2,48,64,128]{3,2,1,0:T(8,128)(2,1)}, u32[]{:S(2)}, u32[]{:S(2)}) %collective-permute-start.3) | collective-permute-done | bytes 1572896 | tf_op jit(solution)/shard_map/ppermute | solution.py:36
  52.9 2.3 fusion.137
  58.3 2.1 fusion.131
  63.6 2.3 fusion.125
  69.0 2.1 fusion.119
  72.5 4.0 collective-permute-start.4
  76.5 2.3 fusion.46
  82.1 2.2 fusion.31
  84.3 2.3 fusion.19
  86.6 4.9 add_divide_fusion
  93.0 4.4 collective-permute-start.6
  103.4 2.3 broadcast_select_fusion
  110.1 14.3 %all-reduce.5 = (f32[1,24,24]{2,1,0:T(8,128)S(1)}, f32[1,24]{1,0:T(1,128)S(1)}) all-reduce(f32[1,24,24]{2,1,0:T(8,128)S(1)} %fusion.97, f32[1,24]{1,0:T(1,128)S(1)} %fusion.106), channel_id=1, replica_groups=mesh['edge'=64,'pix'=4] {'pix'}, use_global_device_ids=true, to_apply=%region_9.10 | all-reduce | flops 600 | bytes 4800 | tf_op jit(solution)/shard_map/psum | solution.py:239
  124.4 59.8 %all_gather.6 = f32[64,24,24]{2,1,0:T(8,128)S(1)} all-gather(f32[1,24,24]{2,1,0:T(8,128)S(1)} %get-tuple-element.36), channel_id=1, replica_groups=mesh['edge'=64,'pix'=4] {'edge'}, dimensions={0}, use_global_device_ids=true | all-gather | bytes 149760 | tf_op jit(solution)/shard_map/all_gather | solution.py:241
  185.9 12.3 %fusion = f32[64,12,64,12]{1,0,3,2:T(8,128)} fusion(f32[64,64]{0,1:T(8,128)S(1)} %get-tuple-element.125, f32[64,12,12]{1,0,2:T(8,128)S(1)} %copy.62, f32[64,64]{0,1:T(8,128)S(1)} %get-tuple-element.124, f32[64,12,12]{1,0,2:T(8,128)S(1)} %copy.61), kind=kLoop, calls=%fused_computation.4 | loop fusion | flops 1769472 | bytes 2465792 | tf_op jit(solution)/shard_map/add | solution.py:174
  198.2 33.5 %copy.63 = f32[64,12,64,12]{3,2,1,0:T(8,128)} copy(f32[64,12,64,12]{1,0,3,2:T(8,128)} %fusion) | data formatting | bytes 4718592 | tf_op jit(solution)/shard_map/add | solution.py:174
  231.7 18.1 %fusion.1 = f32[64,12,64,12]{3,2,1,0:T(8,128)} fusion(f32[64,12,64,12]{3,2,1,0:T(8,128)} %copy.63, f32[64,64]{0,1:T(8,128)S(1)} %get-tuple-element.125, f32[64,12,12]{1,0,2:T(8,128)S(1)} %copy.62), kind=kLoop, calls=%fused_computation.5 | loop fusion | flops 1179648 | bytes 4771840 | tf_op jit(solution)/shard_map/add | solution.py:174
  249.8 22.7 %reshape.435 = f32[768,768]{1,0:T(8,128)} reshape(f32[64,12,64,12]{3,2,1,0:T(8,128)} %fusion.1) | data formatting | bytes 4718592 | tf_op jit(solution)/shard_map/reshape | solution.py:176
  272.5 2.0 copy.64
  276.1 3.2 copy.65
  279.3 2.1 fusion.18
  282.9 11.7 %cholesky.164 = f32[128,128]{1,0:T(8,128)S(1)} custom-call(f32[128,128]{1,0:T(8,128)S(1)} %cholesky.421), custom_call_target="Cholesky" | custom-call | tf_op jit(solution)/shard_map/jit(cholesky)/cholesky | solution.py:181
  294.7 9.8 %custom-call.48 = f32[1,128,128]{1,2,0:T(8,128)S(1)} custom-call(f32[1,128,128]{2,1,0:T(8,128)S(1)} %get-tuple-element.60), custom_call_target="InvertDiagBlocksLowerTriangular" | custom-call | tf_op jit(solution)/shard_map/jit(cholesky)/cholesky | solution.py:181
  307.5 11.7 %cholesky.187 = f32[128,128]{1,0:T(8,128)S(1)} custom-call(f32[128,128]{1,0:T(8,128)S(1)} %cholesky.425), custom_call_target="Cholesky" | custom-call | tf_op jit(solution)/shard_map/jit(cholesky)/cholesky | solution.py:181
  319.4 10.2 %custom-call.49 = f32[1,128,128]{1,2,0:T(8,128)S(1)} custom-call(f32[1,128,128]{2,1,0:T(8,128)S(1)} %get-tuple-element.58), custom_call_target="InvertDiagBlocksLowerTriangular" | custom-call | tf_op jit(solution)/shard_map/jit(cholesky)/cholesky | solution.py:181
  330.2 2.0 convolution_subtract_fusion.1
  332.2 11.7 %cholesky.352 = f32[128,128]{1,0:T(8,128)S(1)} custom-call(f32[128,128]{1,0:T(8,128)S(1)} %cholesky.430), custom_call_target="Cholesky" | custom-call | tf_op jit(solution)/shard_map/jit(cholesky)/cholesky | solution.py:181
  344.1 9.8 %custom-call.50 = f32[1,128,128]{1,2,0:T(8,128)S(1)} custom-call(f32[1,128,128]{2,1,0:T(8,128)S(1)} %get-tuple-element.56), custom_call_target="InvertDiagBlocksLowerTriangular" | custom-call | tf_op jit(solution)/shard_map/jit(cholesky)/cholesky | solution.py:181
  354.3 2.1 convolution_subtract_fusion.2
  356.4 11.9 %cholesky.371 = f32[128,128]{1,0:T(8,128)S(1)} custom-call(f32[128,128]{1,0:T(8,128)S(1)} %cholesky.435), custom_call_target="Cholesky" | custom-call | tf_op jit(solution)/shard_map/jit(cholesky)/cholesky | solution.py:181
  368.4 9.8 %custom-call.51 = f32[1,128,128]{1,2,0:T(8,128)S(1)} custom-call(f32[1,128,128]{2,1,0:T(8,128)S(1)} %get-tuple-element.54), custom_call_target="InvertDiagBlocksLowerTriangular" | custom-call | tf_op jit(solution)/shard_map/jit(cholesky)/cholesky | solution.py:181
  378.6 1.9 convolution_subtract_fusion.3
  380.5 11.7 %cholesky.390 = f32[128,128]{1,0:T(8,128)S(1)} custom-call(f32[128,128]{1,0:T(8,128)S(1)} %cholesky.440), custom_call_target="Cholesky" | custom-call | tf_op jit(solution)/shard_map/jit(cholesky)/cholesky | solution.py:181
  392.3 9.8 %custom-call.52 = f32[1,128,128]{1,2,0:T(8,128)S(1)} custom-call(f32[1,128,128]{2,1,0:T(8,128)S(1)} %get-tuple-element.52), custom_call_target="InvertDiagBlocksLowerTriangular" | custom-call | tf_op jit(solution)/shard_map/jit(cholesky)/cholesky | solution.py:181
  404.2 11.7 %cholesky.408 = f32[128,128]{1,0:T(8,128)S(1)} custom-call(f32[128,128]{1,0:T(8,128)S(1)} %convolution_subtract_fusion.4), custom_call_target="Cholesky" | custom-call | tf_op jit(solution)/shard_map/jit(cholesky)/cholesky | solution.py:181
  420.0 37.3 %all-gather = f32[64,1,24]{2,1,0:T(1,128)S(1)} all-gather(f32[1,1,24]{2,1,0:T(1,128)S(1)} %bitcast.562), channel_id=1, replica_groups=mesh['edge'=64,'pix'=4] {'edge'}, dimensions={0}, use_global_device_ids=true | all-gather | bytes 6240 | tf_op jit(solution)/shard_map/all_gather | solution.py:242
  463.0 21.6 %while.1 = (s32[]{:T(128)}, f32[768,768]{0,1:T(8,128)}, s32[6,2]{0,1:T(2,128)S(1)}, f32[6,128,128]{2,1,0:T(8,128)}, s32[]{:T(128)}) while((s32[]{:T(128)}, f32[768,768]{0,1:T(8,128)}, s32[6,2]{0,1:T(2,128)S(1)}, f32[6,128,128]{2,1,0:T(8,128)}, s32[]{:T(128)}) %tuple.82), condition=%wide.while_cond, body=%wide.while_body.sunk | while | flops 2 | bytes 393329 | solution.py:157
  463.5 2.3 dynamic-slice.7
  467.2 2.3 dynamic-slice.7
  470.8 2.3 dynamic-slice.7
  474.4 2.3 dynamic-slice.7
  478.0 2.3 dynamic-slice.7
  481.6 2.2 dynamic-slice.7
  484.6 59.8 %custom-call.53 = f32[6,128,128]{1,2,0:T(8,128)S(1)} custom-call(f32[6,128,128]{2,1,0:T(8,128)} %get-tuple-element.10), custom_call_target="InvertDiagBlocksLowerTriangular" | custom-call | tf_op jit(solution)/shard_map/triangular_solve | solution.py:157
  (225 shorter events, 79.9 us)
Async XLA Ops:
  0.6 4.3 copy-start
  0.6 23.4 %copy-start.4 = (bf16[2,12,64,128]{3,2,1,0:T(8,128)(2,1)S(1)}, bf16[2,12,64,128]{3,2,1,0:T(8,128)(2,1)}, u32[]{:S(2)}) copy-start(bf16[2,12,64,128]{3,2,1,0:T(8,128)(2,1)} %param.9) | copy-start | bytes 1179652
  0.7 10.1 %collective-permute-start = (bf16[2,12,64,128]{3,2,1,0:T(8,128)(2,1)}, bf16[2,12,64,128]{3,2,1,0:T(8,128)(2,1)S(1)}, u32[]{:S(2)}, u32[]{:S(2)}) collective-permute-start(bf16[2,12,64,128]{3,2,1,0:T(8,128)(2,1)} %param.9), channel_id=1, source_target_pairs={{0,1},{1,2},{2,3},{3,0},{4,5},{5,6},{6,7},{7,4},{8,9},{9,10},{10,1... | collective-permute-start | bytes 1179656 | tf_op jit(solution)/shard_map/ppermute | solution.py:21
  2.8 21.4 %collective-permute-start.1 = (bf16[2,12,64,128]{3,2,1,0:T(8,128)(2,1)}, bf16[2,12,64,128]{3,2,1,0:T(8,128)(2,1)S(1)}, u32[]{:S(2)}, u32[]{:S(2)}) collective-permute-start(bf16[2,12,64,128]{3,2,1,0:T(8,128)(2,1)} %param.9), channel_id=1, source_target_pairs={{0,3},{1,0},{2,1},{3,2},{4,7},{5,4},{6,5},{7,6},{8,11},{9,8},{10,9... | collective-permute-start | bytes 1179656 | tf_op jit(solution)/shard_map/ppermute | solution.py:26
  4.9 24.3 %copy-start.8 = (s32[4]{0:T(128)}, s32[4]{0:T(128)S(1)}, u32[]{:S(2)}) copy-start(s32[4]{0:T(128)S(1)} %get-tuple-element.78) | copy-start | bytes 52
  10.8 13.5 %collective-permute-start.2 = (bf16[2,12,64,128]{3,2,1,0:T(8,128)(2,1)S(1)}, bf16[2,12,64,128]{3,2,1,0:T(8,128)(2,1)S(1)}, u32[]{:S(2)}, u32[]{:S(2)}) collective-permute-start(bf16[2,12,64,128]{3,2,1,0:T(8,128)(2,1)S(1)} %collective-permute-done), channel_id=1, source_target_pairs={{0,1},{1,2},{2,3},{3,0},{4,5},{5,6},{6,7},{7,4},{8,9},{9,10},{10,1... | collective-permute-start | bytes 1179656 | tf_op jit(solution)/shard_map/ppermute | solution.py:21
  24.4 23.7 %collective-permute-start.3 = (bf16[2,48,64,128]{3,2,1,0:T(8,128)(2,1)S(1)}, bf16[2,48,64,128]{3,2,1,0:T(8,128)(2,1)}, u32[]{:S(2)}, u32[]{:S(2)}) collective-permute-start(bf16[2,48,64,128]{3,2,1,0:T(8,128)(2,1)S(1)} %constant_dynamic-update-slice_fusion.28), channel_id=1, source_target_pairs={{4,0},{8,4},{12,8},{16,12},{20,16},{24,20},{28,24},{32,28},{36,32}... | collective-permute-start | bytes 4718600 | tf_op jit(solution)/shard_map/ppermute | solution.py:36
  69.0 2.1 copy-start.2
  69.0 7.5 %copy-start.5 = (bf16[9,256,256]{2,1,0:T(8,128)(2,1)S(1)}, bf16[9,256,256]{2,1,0:T(8,128)(2,1)}, u32[]{:S(2)}) copy-start(bf16[9,256,256]{2,1,0:T(8,128)(2,1)} %param.15) | copy-start | bytes 3538948
  71.2 7.6 %collective-permute-start.5 = (bf16[4,1,64,256]{3,2,1,0:T(8,128)(2,1)S(1)}, bf16[4,1,64,256]{3,2,1,0:T(8,128)(2,1)S(1)}, u32[]{:S(2)}, u32[]{:S(2)}) collective-permute-start(bf16[4,1,64,256]{3,2,1,0:T(8,128)(2,1)S(1)} %get-tuple-element.45), channel_id=1, source_target_pairs={{1,0},{2,1},{3,2},{5,4},{6,5},{7,6},{9,8},{10,9},{11,10},{13,12},{... | collective-permute-start | bytes 393224 | tf_op jit(solution)/shard_map/ppermute | solution.py:49
  72.5 6.3 %collective-permute-start.4 = (bf16[4,1,64,256]{3,2,1,0:T(8,128)(2,1)S(1)}, bf16[4,1,64,256]{3,2,1,0:T(8,128)(2,1)S(1)}, u32[]{:S(2)}, u32[]{:S(2)}) collective-permute-start(bf16[4,1,64,256]{3,2,1,0:T(8,128)(2,1)S(1)} %get-tuple-element.44), channel_id=1, source_target_pairs={{0,1},{1,2},{2,3},{4,5},{5,6},{6,7},{8,9},{9,10},{10,11},{12,13},{... | collective-permute-start | bytes 393224 | tf_op jit(solution)/shard_map/ppermute | solution.py:47
  91.7 6.0 %collective-permute-start.7 = (bf16[4,1,64,128]{3,2,1,0:T(8,128)(2,1)S(1)}, bf16[4,1,64,128]{3,2,1,0:T(8,128)(2,1)S(1)}, u32[]{:S(2)}, u32[]{:S(2)}) collective-permute-start(bf16[4,1,64,128]{3,2,1,0:T(8,128)(2,1)S(1)} %get-tuple-element.49), channel_id=1, source_target_pairs={{1,0},{2,1},{3,2},{5,4},{6,5},{7,6},{9,8},{10,9},{11,10},{13,12},{... | collective-permute-start | bytes 196616 | tf_op jit(solution)/shard_map/ppermute | solution.py:49
  93.0 5.4 collective-permute-start.6
  97.5 1.2 copy-start.6
  102.8 0.7 copy-start.11
  103.4 2.3 copy-start.10
  103.4 2.6 copy-start.7
  103.4 2.8 copy-start.9
  281.5 1.4 copy-start.3
  461.3 1.6 copy-start.12
  463.0 97.4 %copy-start.1 = (f32[2,768]{1,0:T(2,128)S(1)}, f32[2,768]{1,0:T(2,128)}, u32[]{:S(2)}) copy-start(f32[2,768]{1,0:T(2,128)} %param.11) | copy-start | bytes 18436
